TPU v7x, 32 devices: a whole 2x2x4 slice. The times are simulated.
32 devices in a mesh: group: 4 (over y, core), tile: 8 (over z, x).
Axes of the slice: x: 2, y: 2, z: 4, core: 2. Of those that a mesh axis runs over, the one named last changes fastest.
Arguments:
- features: bfloat16 [65536, 128], P(('group', 'tile')), may hold values from -6 to 6
- kernel_map: int32 [32, 27, 2048], P(('group', 'tile')), may hold values from 0 to 2560, as said below
- send_order: int32 [32, 2048], P(('group', 'tile')), may hold values from 0 to 2047, each once within a row
- counts: int32 [32], P(('group', 'tile')), may hold values from 1 to 2048, 49152 in all
- first_weight: bfloat16 [27, 128, 128], replicated, may hold values from -0.109375 to 0.109375
- second_weight: bfloat16 [27, 128, 128], replicated, may hold values from -0.109375 to 0.109375
- norm_gain: float32 [128], replicated, may hold values from 0.1 to 1.9
- cotangent: bfloat16 [65536, 128], P(('group', 'tile')), may hold values from -6 to 6
Outputs:
- serial_out: bfloat16 [65536, 128], P(('group', 'tile'))
- grad_features: bfloat16 [65536, 128], P(('group', 'tile'))
- first_grad: float32 [27, 128, 128], replicated
- second_grad: float32 [27, 128, 128], replicated
- gain_grad: float32 [128], replicated
Inputs may be any that keep to these rules, and one draw needn't show every extreme that they name: `kernel_map`: entry [d, k, i] is the row of tile d's table read by voxel slot i for offset k: rows 0 to 255 are the previous tile's slots 256 to 511, then the tile's own 2048 slots, then the next tile's first 256 slots, and 2560 means no neighbour. Offset 13 is the voxel itself. Only slots below 256 read the previous tile, only slots 256 to 511 read the next. `send_order`: each row holds every slot once. `counts`: the largest is exactly 2048.
All inputs are finite; a program needn't handle non-finite values. No bound on the sum of `counts` on one device may be relied on, other than what follows from the above.
Results may differ from a plain program's by a relative error of at most 0.0049.
Values may be sent and summed in bfloat16 or wider, within the bound.
No kernel may reach another device: no remote copies, remote signals or barrier semaphores. Data moves between devices by JAX's collectives and lax.ppermute only.
A program may use at most 192 MiB of HBM per device.

v0:
```python
import jax
import jax.numpy as jnp
from jax import lax
from jax.sharding import PartitionSpec as P

F = 256


def shifted(value, axis, steps):
    count = lax.axis_size(axis)
    initial, last = (max(0, -steps), min(count, count - steps))
    return lax.ppermute(value, axis, [(source, source + steps) for source in range(initial, last)])


def extend(field):
    chans = field.shape[1]
    before = shifted(field[F : 2 * F], ("group", "tile"), 1)
    after = shifted(field[:F], ("group", "tile"), -1)
    zero_row = jnp.zeros((1, chans), field.dtype)
    return jnp.concatenate([before, field, after, zero_row], axis=0)


def fold_table(table_grad):
    slots = table_grad.shape[0] - 2 * F - 1
    own = table_grad[F : F + slots]
    from_prev = shifted(
        table_grad[slots + F : slots + 2 * F].astype(jnp.bfloat16), ("group", "tile"), 1
    ).astype(jnp.float32)
    from_next = shifted(table_grad[:F].astype(jnp.bfloat16), ("group", "tile"), -1).astype(
        jnp.float32
    )
    own = own.at[:F].add(from_prev)
    own = own.at[F : 2 * F].add(from_next)
    return own


def gather_rows(table, neighbours):
    slots = neighbours.shape[1]
    offsets = neighbours.shape[0]
    rows = jnp.take(table, neighbours.T, axis=0)
    return rows.reshape(slots, offsets * table.shape[1])


def convolve(table, neighbours, weights):
    offsets, chans_in, chans = weights.shape
    gathered = gather_rows(table, neighbours)
    return jnp.dot(
        gathered, weights.reshape(offsets * chans_in, chans), preferred_element_type=jnp.float32
    )


def convolve_back(table, neighbours, weights, grad_out):
    offsets, chans_in, chans = weights.shape
    slots = neighbours.shape[1]
    gathered = gather_rows(table, neighbours)
    weight_term = lax.dot_general(
        gathered, grad_out, (((0,), (0,)), ((), ())), preferred_element_type=jnp.float32
    )
    terms = lax.dot_general(
        grad_out,
        weights.reshape(offsets * chans_in, chans),
        (((1,), (1,)), ((), ())),
        preferred_element_type=jnp.float32,
    )
    terms = terms.reshape(slots * offsets, chans_in)
    table_grad = jax.ops.segment_sum(terms, neighbours.T.reshape(-1), num_segments=table.shape[0])
    return (weight_term.reshape(offsets, chans_in, chans), table_grad)


def norm_act(first, gain, live):
    centre = jnp.mean(first, axis=-1, keepdims=True)
    centred = first - centre
    variance = jnp.mean(centred * centred, axis=-1, keepdims=True)
    inv_std = lax.rsqrt(variance + 1e-05)
    unit = centred * inv_std
    normed = unit * gain
    hidden = (jax.nn.gelu(normed) * live).astype(jnp.bfloat16)
    return (hidden, unit, inv_std, normed)


def norm_back(grad_hidden, normed, unit, inv_std, gain, live):
    _, pull = jax.vjp(jax.nn.gelu, normed)
    grad_normed = pull(grad_hidden * live)[0]
    gain_term = jnp.sum(grad_normed * unit, axis=0)
    grad_unit = grad_normed * gain
    centred_grad = (
        grad_unit
        - jnp.mean(grad_unit, axis=-1, keepdims=True)
        - unit * jnp.mean(grad_unit * unit, axis=-1, keepdims=True)
    )
    return ((inv_std * centred_grad).astype(jnp.bfloat16), gain_term)


def to_serial(rows):
    return lax.all_to_all(rows, ("group", "tile"), split_axis=0, concat_axis=0, tiled=True)


def to_spatial(rows):
    return lax.all_to_all(rows, ("group", "tile"), split_axis=0, concat_axis=0, tiled=True)


def local(
    features, kernel_map, send_order, counts, first_weight, second_weight, norm_gain, cotangent
):
    slots, chans = features.shape
    neighbours = kernel_map[0]
    order = send_order[0]
    live = (jnp.arange(slots, dtype=jnp.int32) < counts[0]).astype(jnp.float32)[:, None]
    masked = (features.astype(jnp.float32) * live).astype(jnp.bfloat16)
    table_x = extend(masked)
    first = convolve(table_x, neighbours, first_weight)
    hidden, unit, inv_std, normed = norm_act(first, norm_gain, live)
    table_h = extend(hidden)
    second = convolve(table_h, neighbours, second_weight)
    block = ((masked.astype(jnp.float32) + second) * live).astype(jnp.bfloat16)
    ordered = jnp.take(block, order, axis=0)
    serial_out = to_serial(ordered)
    slotted = to_spatial(cotangent)
    grad_block = jnp.zeros_like(slotted).at[order].set(slotted)
    grad_live = (grad_block.astype(jnp.float32) * live).astype(jnp.bfloat16)
    second_term, table_grad_h = convolve_back(table_h, neighbours, second_weight, grad_live)
    grad_hidden = fold_table(table_grad_h)
    grad_first, gain_term = norm_back(grad_hidden, normed, unit, inv_std, norm_gain, live)
    first_term, table_grad_x = convolve_back(table_x, neighbours, first_weight, grad_first)
    grad_x = fold_table(table_grad_x) + grad_live.astype(jnp.float32)
    grad_features = (grad_x * live).astype(jnp.bfloat16)
    first_grad, second_grad, gain_grad = lax.psum(
        (first_term, second_term, gain_term), ("group", "tile")
    )
    return (serial_out, grad_features, first_grad, second_grad, gain_grad)


def solution(mesh):
    placed = (
        P(("group", "tile"), None),
        P(("group", "tile"), None, None),
        P(("group", "tile"), None),
        P(("group", "tile")),
        P(),
        P(),
        P(),
        P(("group", "tile"), None),
    )
    return jax.shard_map(
        local,
        mesh=mesh,
        in_specs=placed,
        out_specs=(P(("group", "tile"), None), P(("group", "tile"), None), P(), P(), P()),
        check_vma=False,
    )
```

profile of v0, /device:TPU:0, one launch (start us, length us, event | category | flops | bytes accessed | tf_op | source)
XLA Modules:
  0.0 1434.9 jit_solution(7541587480908522428)
XLA Ops:
  7.2 7.4 all-to-all-start.1
  17.4 3.6 collective-permute-start
  33.7 192.0 %gather_fusion.1 = bf16[55296,128]{1,0:T(8,128)(2,1)} fusion(bf16[2561,128]{1,0:T(8,128)(2,1)S(1)} %maximum_maximum_fusion, s32[55296]{0:T(1024)S(1)} %broadcast_clamp_fusion), kind=kCustom, calls=%fused_computation.clone | custom fusion | bytes 28532736 | tf_op jit(solution)/shard_map/jit(_take)/gather | solution.py:40
  225.6 22.4 %reshape.269 = bf16[2048,27,128]{2,1,0:T(8,128)(2,1)} reshape(bf16[55296,128]{1,0:T(8,128)(2,1)} %gather_fusion.1) | data formatting | bytes 28311552 | tf_op jit(solution)/shard_map/jit(_take)/gather | solution.py:40
  248.1 13.4 broadcast_select_fusion
  261.5 23.6 %copy.22 = bf16[2048,27,128]{0,2,1:T(8,128)(2,1)} copy(bf16[2048,27,128]{2,1,0:T(8,128)(2,1)} %broadcast_select_fusion) | data formatting | bytes 28311552 | tf_op jit(solution)/shard_map/jit(_take)/select_n | solution.py:40
  285.1 7.3 fusion.32
  294.1 6.4 scatter_custom_fusion
  300.5 11.4 fusion.26
  311.9 28.8 %reshape.248 = f32[55296,128]{1,0:T(8,128)} reshape(f32[2048,3456]{1,0:T(8,128)} %fusion.26) | data formatting | bytes 56623104 | tf_op jit(solution)/shard_map/reshape | solution.py:65
  340.7 293.6 %scatter_custom_fusion.1 = f32[2561,128]{1,0:T(8,128)S(1)} fusion(s32[55296]{0:T(1024)} %reshape.254, f32[55296,128]{1,0:T(8,128)} %reshape.248, f32[]{:T(128)} %constant.138.clone.1), kind=kCustom, calls=%fused_computation.40 | custom fusion | flops 7077888 | bytes 1311744 | tf_op jit(solution)/shard_map/scatter-add | solution.py:66
  634.4 4.6 collective-permute-start.4
  641.2 5.3 collective-permute-done.5
  646.6 2.9 multiply_reduce_fusion
  650.9 3.8 collective-permute-start.2
  656.3 10.7 fusion.2
  667.0 11.7 fusion.33
  678.8 28.8 %reshape.256 = f32[55296,128]{1,0:T(8,128)} reshape(f32[2048,3456]{1,0:T(8,128)} %fusion.33) | data formatting | bytes 56623104 | tf_op jit(solution)/shard_map/reshape | solution.py:65
  707.6 293.6 %scatter_custom_fusion.2 = f32[2561,128]{1,0:T(8,128)S(1)} fusion(s32[55296]{0:T(1024)} %reshape.254, f32[55296,128]{1,0:T(8,128)} %reshape.256, f32[]{:T(128)} %constant.138.clone.1), kind=kCustom, calls=%fused_computation.38 | custom fusion | flops 7077888 | bytes 1311744 | tf_op jit(solution)/shard_map/scatter-add | solution.py:66
  1001.9 4.8 collective-permute-start.6
  1008.1 192.0 %gather_fusion.2 = bf16[55296,128]{1,0:T(8,128)(2,1)} fusion(bf16[2561,128]{1,0:T(8,128)(2,1)S(1)} %maximum_maximum_fusion.1, s32[55296]{0:T(1024)S(1)} %broadcast_clamp_fusion), kind=kCustom, calls=%fused_computation.1.clone | custom fusion | bytes 28532736 | tf_op jit(solution)/shard_map/jit(_take)/gather | solution.py:40
  1200.1 22.4 %reshape.273 = bf16[2048,27,128]{2,1,0:T(8,128)(2,1)} reshape(bf16[55296,128]{1,0:T(8,128)(2,1)} %gather_fusion.2) | data formatting | bytes 28311552 | tf_op jit(solution)/shard_map/jit(_take)/gather | solution.py:40
  1222.5 13.4 broadcast_select_fusion.1
  1235.9 23.5 %copy.23 = bf16[2048,27,128]{0,2,1:T(8,128)(2,1)} copy(bf16[2048,27,128]{2,1,0:T(8,128)(2,1)} %broadcast_select_fusion.1) | data formatting | bytes 28311552 | tf_op jit(solution)/shard_map/jit(_take)/select_n | solution.py:40
  1259.5 8.5 fusion
  1268.0 9.5 fusion.6
  1277.5 8.1 gather_fusion
  1287.7 10.6 all-to-all-start
  1300.6 42.6 %psum.23 = f32[128]{0:T(128)} all-reduce(f32[128]{0:T(128)S(1)} %get-tuple-element.54), channel_id=1, replica_groups=mesh['group'=4,'tile'=8] {'group','tile'}, use_global_device_ids=true, to_apply=%region_10.12 | all-reduce | flops 128 | bytes 1024 | tf_op jit(solution)/shard_map/psum | solution.py:127
  1348.0 73.6 %all-reduce.3.cloned.1.call-done = (f32[27,128,128]{2,1,0:T(8,128)}, f32[27,128,128]{2,1,0:T(8,128)}) async-done(((f32[27,128,128]{2,1,0:T(8,128)}, f32[27,128,128]{2,1,0:T(8,128)}), (f32[27,128,128]{2,1,0:T(8,128)}, f32[27,128,128]{2,1,0:T(8,128)})) %all-reduce.3.cloned.1.call-update) | async-done | bytes 3538960 | tf_op jit(solution)/shard_map/psum | solution.py:127
  1422.3 2.9 copy.38
  1425.2 2.9 copy.39
  (75 shorter events, 33.8 us)
Async XLA Ops:
  7.2 277.9 %copy-start = (bf16[27,128,128]{2,1,0:T(8,128)(2,1)S(1)}, bf16[27,128,128]{2,1,0:T(8,128)(2,1)}, u32[]{:S(2)}) copy-start(bf16[27,128,128]{2,1,0:T(8,128)(2,1)} %param.22) | copy-start | bytes 2654212
  7.2 286.9 %all-to-all-start.1 = ((bf16[32,64,128]{2,1,0:T(8,128)(2,1)}), bf16[32,64,128]{2,1,0:T(8,128)(2,1)}, u32[]{:S(2)}, u32[]{:S(2)}) async-start(bf16[32,64,128]{2,1,0:T(8,128)(2,1)} %bitcast.61), calls=%async_computation.1 | async-start | bytes 1048576 | tf_op jit(solution)/shard_map/all_to_all | solution.py:99
  14.6 1406.9 %all-reduce.3.cloned.1.call-start = ((), (), s32[]{:S(2)}) async-start(), calls=%async_computation.2 | async-start | bytes 7077888 | tf_op jit(solution)/shard_map/psum | solution.py:127
  17.4 15.9 %collective-permute-start = (bf16[256,128]{1,0:T(8,128)(2,1)}, bf16[256,128]{1,0:T(8,128)(2,1)S(1)}, u32[]{:S(2)}, u32[]{:S(2)}) collective-permute-start(bf16[256,128]{1,0:T(8,128)(2,1)} %get-tuple-element.67), channel_id=1, source_target_pairs={{0,1},{1,2},{2,3},{3,4},{4,5},{5,6},{6,7},{7,8},{8,9},{9,10},{10,1... | collective-permute-start | bytes 196616 | tf_op jit(solution)/shard_map/ppermute | solution.py:12
  21.0 12.3 collective-permute-start.1
  225.6 22.5 %copy-start.6 = (pred[2048,27]{1,0:T(8,128)(4,1)S(1)}, pred[2048,27]{1,0:T(8,128)(4,1)}, u32[]{:S(2)}) copy-start(pred[2048,27]{1,0:T(8,128)(4,1)} %copy.15) | copy-start | bytes 165892
  285.1 15.4 %copy-start.7 = (bf16[27,128,128]{2,1,0:T(8,128)(2,1)S(1)}, bf16[27,128,128]{2,1,0:T(8,128)(2,1)}, u32[]{:S(2)}) copy-start(bf16[27,128,128]{2,1,0:T(8,128)(2,1)} %param.23) | copy-start | bytes 2654212
  292.4 1.0 copy-start.2
  300.4 959.0 %copy-start.4 = (bf16[2048,128]{1,0:T(8,128)(2,1)}, bf16[2048,128]{1,0:T(8,128)(2,1)S(1)}, u32[]{:S(2)}) copy-start(bf16[2048,128]{1,0:T(8,128)(2,1)S(1)} %scatter_custom_fusion) | copy-start | bytes 1572868
  311.9 334.7 %copy-start.10 = (f32[128]{0:T(128)S(1)}, f32[128]{0:T(128)}, u32[]{:S(2)}) copy-start(f32[128]{0:T(128)} %param.24) | copy-start | bytes 1540
  634.4 6.8 collective-permute-start.4
  639.1 7.5 collective-permute-start.5
  649.5 0.8 copy-start.5
  649.5 17.5 %copy-start.3 = (f32[2048,128]{1,0:T(8,128)S(1)}, f32[2048,128]{1,0:T(8,128)}, u32[]{:S(2)}) copy-start(f32[2048,128]{1,0:T(8,128)} %copy-done.2) | copy-start | bytes 3145732
  650.9 355.8 %collective-permute-start.2 = (bf16[256,128]{1,0:T(8,128)(2,1)}, bf16[256,128]{1,0:T(8,128)(2,1)S(1)}, u32[]{:S(2)}, u32[]{:S(2)}) collective-permute-start(bf16[256,128]{1,0:T(8,128)(2,1)} %get-tuple-element.65), channel_id=1, source_target_pairs={{0,1},{1,2},{2,3},{3,4},{4,5},{5,6},{6,7},{7,8},{8,9},{9,10},{10,1... | collective-permute-start | bytes 196616 | tf_op jit(solution)/shard_map/ppermute | solution.py:12
  654.8 351.9 %collective-permute-start.3 = (bf16[256,128]{1,0:T(8,128)(2,1)}, bf16[256,128]{1,0:T(8,128)(2,1)S(1)}, u32[]{:S(2)}, u32[]{:S(2)}) collective-permute-start(bf16[256,128]{1,0:T(8,128)(2,1)} %get-tuple-element.66), channel_id=1, source_target_pairs={{1,0},{2,1},{3,2},{4,3},{5,4},{6,5},{7,6},{8,7},{9,8},{10,9},{11,1... | collective-permute-start | bytes 196616 | tf_op jit(solution)/shard_map/ppermute | solution.py:12
  1001.9 341.4 %collective-permute-start.6 = (bf16[256,128]{1,0:T(8,128)(2,1)}, bf16[256,128]{1,0:T(8,128)(2,1)S(1)}, u32[]{:S(2)}, u32[]{:S(2)}) collective-permute-start(bf16[256,128]{1,0:T(8,128)(2,1)} %get-tuple-element.62), channel_id=1, source_target_pairs={{0,1},{1,2},{2,3},{3,4},{4,5},{5,6},{6,7},{7,8},{8,9},{9,10},{10,1... | collective-permute-start | bytes 196616 | tf_op jit(solution)/shard_map/ppermute | solution.py:12
  1267.9 9.5 copy-start.8
  1267.9 17.6 %copy-start.9 = (pred[32,64]{1,0:T(8,128)(4,1)S(1)}, pred[32,64]{1,0:T(8,128)(4,1)}, u32[]{:S(2)}) copy-start(pred[32,64]{1,0:T(8,128)(4,1)} %compare_and_fusion.1) | copy-start | bytes 6148
  1268.0 160.1 %copy-start.1 = (bf16[27,128,128]{2,1,0:T(8,128)(2,1)S(1)}, bf16[27,128,128]{2,1,0:T(8,128)(2,1)}, u32[]{:S(2)}) copy-start(bf16[27,128,128]{2,1,0:T(8,128)(2,1)} %param.22) | copy-start | bytes 2654212
  1287.7 60.3 %all-to-all-start = ((bf16[32,64,128]{2,1,0:T(8,128)(2,1)}), bf16[32,64,128]{2,1,0:T(8,128)(2,1)S(1)}, u32[]{:S(2)}, u32[]{:S(2)}) async-start(bf16[32,64,128]{2,1,0:T(8,128)(2,1)} %broadcast_select_fusion.2), calls=%async_computation | async-start | bytes 1048576 | tf_op jit(solution)/shard_map/all_to_all | solution.py:95
  1299.4 44.5 %collective-permute-start.7 = (bf16[256,128]{1,0:T(8,128)(2,1)S(1)}, bf16[256,128]{1,0:T(8,128)(2,1)S(1)}, u32[]{:S(2)}, u32[]{:S(2)}) collective-permute-start(bf16[256,128]{1,0:T(8,128)(2,1)S(1)} %get-tuple-element.61), channel_id=1, source_target_pairs={{1,0},{2,1},{3,2},{4,3},{5,4},{6,5},{7,6},{8,7},{9,8},{10,9},{11,1... | collective-permute-start | bytes 196616 | tf_op jit(solution)/shard_map/ppermute | solution.py:12
Sparse Core Ops, SparseCore 0:
  1268.1 153.4 all-reduce.2
where the time goes:
time: 1440 us; the launch traced here: 1430 us
  other arithmetic  633 us (44%)
  local copies, waits for them, and re-layouts  565 us (39%)
  waiting for transfers between devices  79.8 us (6%)
  matrix products  59.2 us (4%)
  blocking collectives  42.6 us (3%)
  starting transfers between devices  40.2 us (3%)
  between operations  15.1 us (1%)
    scatter-add x2, other arithmetic, convolve_back(): jax.ops.segment_sum(terms, neighbours.T.reshape(-1), num_segments=table.s...  587 us
    gather x4, local copies, waits for them, and re-layouts, gather_rows(): rows = jnp.take(table, neighbours.T, axis=0)  429 us
    psum x1, waiting for transfers between devices, local(): lax.psum((first_term, second_term, gain_term), ('group', 'tile'))  73.6 us
    reshape x2, local copies, waits for them, and re-layouts, convolve_back(): terms = terms.reshape(slots * offsets, chans_in)  57.6 us
    select_n x3, local copies, waits for them, and re-layouts, gather_rows(): rows = jnp.take(table, neighbours.T, axis=0)  47.5 us
    psum x1, blocking collectives, local(): lax.psum((first_term, second_term, gain_term), ('group', 'tile'))  42.6 us
  transfers between devices with their start and end apart: 11, of which 3 were waited for; matrix products, arithmetic and copies ran while one was open for 63% of the time, Pallas kernels for 0%

commit v1 on v0

--- a/solution.py
+++ b/solution.py
@@ -125,7 +125,7 @@
     grad_x = fold_table(table_grad_x) + grad_live.astype(jnp.float32)
     grad_features = (grad_x * live).astype(jnp.bfloat16)
     first_grad, second_grad, gain_grad = lax.psum(
-        (first_term, second_term, gain_term), ("group", "tile")
+        lax.psum((first_term, second_term, gain_term), "tile"), "group"
     )
     return (serial_out, grad_features, first_grad, second_grad, gain_grad)
 

time: 1440 us -> 1370 us (0.951)
  waiting for transfers between devices: 79.8 us -> 27.2 us
    psum x1 -> x2, waiting for transfers between devices: 73.6 us -> 20.9 us  [the longest x1 20.9 us: local(): lax.psum(lax.psum((first_term, second_term, gain_term), 'tile'), 'group')]
    psum x1 -> x2, blocking collectives: 42.6 us -> 29.5 us  [the longest x1 22.9 us: local(): lax.psum((first_term, second_term, gain_term), 'tile')]
  transfers between devices with their start and end apart: 11 -> 12, of which waited for: 3 -> 3; matrix products, arithmetic and copies ran while one was open for 63% -> 47% of each run, Pallas kernels for 0% -> 0%
where the time goes in v1:
time: 1370 us
  other arithmetic  630 us (46%)
  local copies, waits for them, and re-layouts  563 us (41%)
  matrix products  60.7 us (4%)
  starting transfers between devices  40.1 us (3%)
  blocking collectives  29.5 us (2%)
  waiting for transfers between devices  27.2 us (2%)
  between operations  15.1 us (1%)
    scatter-add x2, other arithmetic, convolve_back(): jax.ops.segment_sum(terms, neighbours.T.reshape(-1), num_segments=table.s...  587 us
    gather x4, local copies, waits for them, and re-layouts, gather_rows(): rows = jnp.take(table, neighbours.T, axis=0)  429 us
    reshape x2, local copies, waits for them, and re-layouts, convolve_back(): terms = terms.reshape(slots * offsets, chans_in)  57.7 us
    select_n x3, local copies, waits for them, and re-layouts, gather_rows(): rows = jnp.take(table, neighbours.T, axis=0)  47.7 us
    select_n x3, other arithmetic, gather_rows(): rows = jnp.take(table, neighbours.T, axis=0)  27.8 us
  transfers between devices with their start and end apart: 12, of which 3 were waited for; matrix products, arithmetic and copies ran while one was open for 47% of the time, Pallas kernels for 0%

profile of v1, /device:TPU:0, one launch (start us, length us, event | category | flops | bytes accessed | tf_op | source)
XLA Modules:
  0.0 1365.8 jit_solution(3886909752871877412)
XLA Ops:
  7.2 7.4 all-to-all-start.1
  17.4 3.6 collective-permute-start
  30.5 192.0 %gather_fusion.1 = bf16[55296,128]{1,0:T(8,128)(2,1)} fusion(bf16[2561,128]{1,0:T(8,128)(2,1)S(1)} %maximum_maximum_fusion, s32[55296]{0:T(1024)S(1)} %broadcast_clamp_fusion), kind=kCustom, calls=%fused_computation.clone | custom fusion | bytes 28532736 | tf_op jit(solution)/shard_map/jit(_take)/gather | solution.py:40
  222.5 22.4 %reshape.269 = bf16[2048,27,128]{2,1,0:T(8,128)(2,1)} reshape(bf16[55296,128]{1,0:T(8,128)(2,1)} %gather_fusion.1) | data formatting | bytes 28311552 | tf_op jit(solution)/shard_map/jit(_take)/gather | solution.py:40
  244.9 13.4 broadcast_select_fusion
  258.3 23.6 %copy.22 = bf16[2048,27,128]{0,2,1:T(8,128)(2,1)} copy(bf16[2048,27,128]{2,1,0:T(8,128)(2,1)} %broadcast_select_fusion) | data formatting | bytes 28311552 | tf_op jit(solution)/shard_map/jit(_take)/select_n | solution.py:40
  281.9 7.3 fusion.32
  290.9 6.4 scatter_custom_fusion
  297.3 11.4 fusion.26
  308.8 28.8 %reshape.248 = f32[55296,128]{1,0:T(8,128)} reshape(f32[2048,3456]{1,0:T(8,128)} %fusion.26) | data formatting | bytes 56623104 | tf_op jit(solution)/shard_map/reshape | solution.py:65
  337.6 293.6 %scatter_custom_fusion.1 = f32[2561,128]{1,0:T(8,128)S(1)} fusion(s32[55296]{0:T(1024)} %reshape.254, f32[55296,128]{1,0:T(8,128)} %reshape.248, f32[]{:T(128)} %constant.138.clone.1), kind=kCustom, calls=%fused_computation.40 | custom fusion | flops 7077888 | bytes 1311744 | tf_op jit(solution)/shard_map/scatter-add | solution.py:66
  631.3 4.6 collective-permute-start.4
  638.1 5.3 collective-permute-done.5
  646.4 3.8 collective-permute-start.2
  651.8 10.7 fusion.2
  662.9 192.0 %gather_fusion.2 = bf16[55296,128]{1,0:T(8,128)(2,1)} fusion(bf16[2561,128]{1,0:T(8,128)(2,1)S(1)} %maximum_maximum_fusion.1, s32[55296]{0:T(1024)S(1)} %broadcast_clamp_fusion), kind=kCustom, calls=%fused_computation.1.clone | custom fusion | bytes 28532736 | tf_op jit(solution)/shard_map/jit(_take)/gather | solution.py:40
  854.9 22.4 %reshape.273 = bf16[2048,27,128]{2,1,0:T(8,128)(2,1)} reshape(bf16[55296,128]{1,0:T(8,128)(2,1)} %gather_fusion.2) | data formatting | bytes 28311552 | tf_op jit(solution)/shard_map/jit(_take)/gather | solution.py:40
  877.3 13.4 broadcast_select_fusion.1
  890.6 23.7 %copy.23 = bf16[2048,27,128]{0,2,1:T(8,128)(2,1)} copy(bf16[2048,27,128]{2,1,0:T(8,128)(2,1)} %broadcast_select_fusion.1) | data formatting | bytes 28311552 | tf_op jit(solution)/shard_map/jit(_take)/select_n | solution.py:40
  914.4 8.6 fusion
  924.5 13.2 fusion.33
  937.8 28.9 %reshape.256 = f32[55296,128]{1,0:T(8,128)} reshape(f32[2048,3456]{1,0:T(8,128)} %fusion.33) | data formatting | bytes 56623104 | tf_op jit(solution)/shard_map/reshape | solution.py:65
  966.7 293.6 %scatter_custom_fusion.2 = f32[2561,128]{1,0:T(8,128)S(1)} fusion(s32[55296]{0:T(1024)} %reshape.254, f32[55296,128]{1,0:T(8,128)} %reshape.256, f32[]{:T(128)} %constant.138.clone.1), kind=kCustom, calls=%fused_computation.38 | custom fusion | flops 7077888 | bytes 1311744 | tf_op jit(solution)/shard_map/scatter-add | solution.py:66
  1260.3 4.5 collective-permute-start.6
  1265.0 9.4 fusion.6
  1274.4 8.1 gather_fusion
  1284.6 10.4 all-to-all-start
  1297.3 22.9 %psum.46 = f32[128]{0:T(128)S(1)} all-reduce(f32[128]{0:T(128)S(1)} %get-tuple-element.54), channel_id=1, replica_groups=mesh['group'=4,'tile'=8] {'tile'}, use_global_device_ids=true, to_apply=%region_12.14 | all-reduce | flops 128 | bytes 1024 | tf_op jit(solution)/shard_map/psum | solution.py:128
  1320.2 6.6 psum.47
  1331.5 20.9 %all-reduce.7.cloned.1.call-done = (f32[27,128,128]{2,1,0:T(8,128)}, f32[27,128,128]{2,1,0:T(8,128)}) async-done(((f32[27,128,128]{2,1,0:T(8,128)}, f32[27,128,128]{2,1,0:T(8,128)}), (f32[27,128,128]{2,1,0:T(8,128)}, f32[27,128,128]{2,1,0:T(8,128)})) %all-reduce.7.cloned.1.call-update) | async-done | bytes 3538960 | tf_op jit(solution)/shard_map/psum | solution.py:127
  1353.2 2.9 copy.40
  1356.1 2.9 copy.41
  (77 shorter events, 32.0 us)
Async XLA Ops:
  7.2 274.8 %copy-start = (bf16[27,128,128]{2,1,0:T(8,128)(2,1)S(1)}, bf16[27,128,128]{2,1,0:T(8,128)(2,1)}, u32[]{:S(2)}) copy-start(bf16[27,128,128]{2,1,0:T(8,128)(2,1)} %param.22) | copy-start | bytes 2654212
  7.2 283.7 %all-to-all-start.1 = ((bf16[32,64,128]{2,1,0:T(8,128)(2,1)}), bf16[32,64,128]{2,1,0:T(8,128)(2,1)}, u32[]{:S(2)}, u32[]{:S(2)}) async-start(bf16[32,64,128]{2,1,0:T(8,128)(2,1)} %bitcast.61), calls=%async_computation.1 | async-start | bytes 1048576 | tf_op jit(solution)/shard_map/all_to_all | solution.py:99
  14.6 1250.3 %all-reduce.5.cloned.1.call-start = ((), (), s32[]{:S(2)}) async-start(), calls=%async_computation.2 | async-start | bytes 7077888 | tf_op jit(solution)/shard_map/psum | solution.py:128
  17.4 12.7 collective-permute-start
  21.0 9.1 collective-permute-start.1
  222.5 22.4 %copy-start.6 = (pred[2048,27]{1,0:T(8,128)(4,1)S(1)}, pred[2048,27]{1,0:T(8,128)(4,1)}, u32[]{:S(2)}) copy-start(pred[2048,27]{1,0:T(8,128)(4,1)} %copy.15) | copy-start | bytes 165892
  281.9 15.4 %copy-start.7 = (bf16[27,128,128]{2,1,0:T(8,128)(2,1)S(1)}, bf16[27,128,128]{2,1,0:T(8,128)(2,1)}, u32[]{:S(2)}) copy-start(bf16[27,128,128]{2,1,0:T(8,128)(2,1)} %param.23) | copy-start | bytes 2654212
  289.3 1.0 copy-start.1
  297.3 11.5 copy-start.3
  308.8 334.7 %copy-start.9 = (f32[128]{0:T(128)S(1)}, f32[128]{0:T(128)}, u32[]{:S(2)}) copy-start(f32[128]{0:T(128)} %param.24) | copy-start | bytes 1540
  631.3 6.8 collective-permute-start.4
  635.9 7.5 collective-permute-start.5
  646.3 16.1 %copy-start.5 = (f32[2048,128]{1,0:T(8,128)}, f32[2048,128]{1,0:T(8,128)S(1)}, u32[]{:S(2)}) copy-start(f32[2048,128]{1,0:T(8,128)S(1)} %get-tuple-element.61) | copy-start | bytes 3145732
  646.4 16.1 %collective-permute-start.2 = (bf16[256,128]{1,0:T(8,128)(2,1)S(1)}, bf16[256,128]{1,0:T(8,128)(2,1)S(1)}, u32[]{:S(2)}, u32[]{:S(2)}) collective-permute-start(bf16[256,128]{1,0:T(8,128)(2,1)S(1)} %get-tuple-element.67), channel_id=1, source_target_pairs={{0,1},{1,2},{2,3},{3,4},{4,5},{5,6},{6,7},{7,8},{8,9},{9,10},{10,1... | collective-permute-start | bytes 196616 | tf_op jit(solution)/shard_map/ppermute | solution.py:12
  650.2 12.3 collective-permute-start.3
  890.6 23.7 %copy-start.4 = (bf16[2048,128]{1,0:T(8,128)(2,1)S(1)}, bf16[2048,128]{1,0:T(8,128)(2,1)}, u32[]{:S(2)}) copy-start(bf16[2048,128]{1,0:T(8,128)(2,1)} %copy-done.3) | copy-start | bytes 1572868
  914.3 9.4 copy-start.8
  914.3 10.2 copy-start.2
  922.9 429.5 %all-reduce.7.cloned.1.call-start = ((), (), s32[]{:S(2)}) async-start(), calls=%async_computation.3 | async-start | bytes 7077888 | tf_op jit(solution)/shard_map/psum | solution.py:127
  1260.3 66.5 %collective-permute-start.6 = (bf16[256,128]{1,0:T(8,128)(2,1)S(1)}, bf16[256,128]{1,0:T(8,128)(2,1)S(1)}, u32[]{:S(2)}, u32[]{:S(2)}) collective-permute-start(bf16[256,128]{1,0:T(8,128)(2,1)S(1)} %get-tuple-element.64), channel_id=1, source_target_pairs={{0,1},{1,2},{2,3},{3,4},{4,5},{5,6},{6,7},{7,8},{8,9},{9,10},{10,1... | collective-permute-start | bytes 196616 | tf_op jit(solution)/shard_map/ppermute | solution.py:12
  1284.6 46.9 %all-to-all-start = ((bf16[32,64,128]{2,1,0:T(8,128)(2,1)}), bf16[32,64,128]{2,1,0:T(8,128)(2,1)S(1)}, u32[]{:S(2)}, u32[]{:S(2)}) async-start(bf16[32,64,128]{2,1,0:T(8,128)(2,1)} %broadcast_select_fusion.2), calls=%async_computation | async-start | bytes 1048576 | tf_op jit(solution)/shard_map/all_to_all | solution.py:95
  1296.0 31.5 %collective-permute-start.7 = (bf16[256,128]{1,0:T(8,128)(2,1)S(1)}, bf16[256,128]{1,0:T(8,128)(2,1)S(1)}, u32[]{:S(2)}, u32[]{:S(2)}) collective-permute-start(bf16[256,128]{1,0:T(8,128)(2,1)S(1)} %get-tuple-element.63), channel_id=1, source_target_pairs={{1,0},{2,1},{3,2},{4,3},{5,4},{6,5},{7,6},{8,7},{9,8},{10,9},{11,1... | collective-permute-start | bytes 196616 | tf_op jit(solution)/shard_map/ppermute | solution.py:12
Sparse Core Ops, SparseCore 0:
  923.1 144.6 all-reduce.4
  1265.1 87.2 all-reduce.6
